TPU v7x, 512 devices: a whole 4x4x16 slice. The times are simulated.
512 devices in a mesh: feat: 32 (over x, y, core), rep: 16 (over z).
Axes of the slice: x: 4, y: 4, z: 16, core: 2. Of those that a mesh axis runs over, the one named last changes fastest.
Arguments:
- feats: bfloat16 [16, 8192, 1024], P('rep', None, 'feat'), may hold values from -6 to 6
- w_self: bfloat16 [1024, 256], P('feat'), may hold values from -0.1875 to 0.1875
- w_neigh: bfloat16 [1024, 256], P('feat'), may hold values from -0.1875 to 0.1875
- bias: float32 [256], replicated, may hold values from -3 to 3
- tile_weight: bfloat16 [16, 32, 3, 128, 128], P('rep'), may hold values from -0.375 to 0.375
- tile_src: int32 [16, 32, 3], P('rep'), may hold values from 0 to 63
- tile_count: int32 [16, 32], P('rep'), may hold values from 1 to 3
- owner_order: int32 [16, 32], P('rep'), may hold values from 0 to 31, each once within a row
- cotangent: bfloat16 [16, 4096, 256], P('rep', 'feat'), may hold values from -6 to 6
Outputs:
- hidden: bfloat16 [16, 4096, 256], P('rep', 'feat')
- grad_self: float32 [1024, 256], P('feat')
- grad_neigh: float32 [1024, 256], P('feat')
All inputs are finite; a program needn't handle non-finite values.
Results may differ from a plain program's by a relative error of at most 0.0055.
Values may be sent and summed in bfloat16 or wider, within the bound.
A program may use at most 64 MiB of HBM per device.

v0:
```python
import jax
import jax.numpy as jnp
from jax import lax
from jax.sharding import PartitionSpec as P


def transposed_product(left, right):
    return lax.dot_general(
        left, right, (((0,), (0,)), ((), ())), preferred_element_type=jnp.float32
    )


def body(feats, w_self, w_neigh, bias, tile_weight, tile_src, tile_count, owner_order, cotangent):
    block_rows = tile_weight.shape[3]
    tile_slots = tile_weight.shape[2]
    columns = feats.shape[2]
    by_block = feats[0].reshape(-1, block_rows, columns)
    in_use = jnp.arange(tile_slots)[None, :] < tile_count[0][:, None]
    masked = jnp.where(in_use[:, :, None, None], tile_weight[0], jnp.zeros((), jnp.bfloat16))
    sources = by_block[tile_src[0]]
    aggregate = jnp.einsum(
        "bkij,bkjc->bic", masked, sources, preferred_element_type=jnp.float32
    ).astype(jnp.bfloat16)
    target_rows = by_block[owner_order[0]].reshape(-1, columns)
    target_mean = aggregate[owner_order[0]].reshape(-1, columns)
    partial_sums = jnp.dot(target_rows, w_self, preferred_element_type=jnp.float32)
    partial_sums = partial_sums + jnp.dot(target_mean, w_neigh, preferred_element_type=jnp.float32)
    preact = lax.psum_scatter(partial_sums, "feat", scatter_dimension=0, tiled=True) + bias
    hidden = jax.nn.silu(preact).astype(jnp.bfloat16)
    squash = jax.nn.sigmoid(preact)
    output_grad = (
        cotangent[0].astype(jnp.float32) * squash * (1.0 + preact * (1.0 - squash))
    ).astype(jnp.bfloat16)
    pieces = lax.all_gather(output_grad, "feat", axis=0, tiled=True)
    grad_self = transposed_product(target_rows, pieces)
    grad_neigh = transposed_product(target_mean, pieces)
    grad_self, grad_neigh = lax.psum((grad_self, grad_neigh), "rep")
    return (hidden[None], grad_self, grad_neigh)


def solution(mesh):
    in_specs = (
        P("rep", None, "feat"),
        P("feat", None),
        P("feat", None),
        P(),
        P("rep", None, None, None, None),
        P("rep", None, None),
        P("rep", None),
        P("rep", None),
        P("rep", "feat", None),
    )
    out_specs = (P("rep", "feat", None), P("feat", None), P("feat", None))
    return jax.shard_map(body, mesh=mesh, in_specs=in_specs, out_specs=out_specs, check_vma=False)
```

profile of v0, /device:TPU:2, one launch (start us, length us, event | category | flops | bytes accessed | tf_op | source)
XLA Modules:
  0.0 341.3 jit_solution(3312335809542064258)
XLA Ops:
  7.2 0.0 reduce-scatter.2.cloned.1.call-start
  7.2 0.7 fusion.20
  7.9 0.7 compare_select_fusion
  8.6 0.7 iota_compare_fusion
  9.3 0.1 copy.18
  9.4 0.1 reshape.130
  9.5 1.2 copy.24
  10.7 0.3 copy.16
  11.0 0.6 gather_fusion
  11.6 0.7 gather_fusion.1
  12.4 3.2 fusion.4
  15.6 0.6 gather_fusion.2
  16.2 0.7 fusion.10
  16.9 2.7 convolution_add_fusion
  19.7 0.0 all-gather.2.cloned.1.call-start
  19.7 109.6 %reduce-scatter.2.cloned.1.call-done = f32[128,256]{1,0:T(8,128)} async-done(((f32[4096,256]{1,0:T(8,128)}), f32[128,256]{1,0:T(8,128)}) %reduce-scatter.2.cloned.1.call-update) | async-done | bytes 131088 | tf_op jit(solution)/shard_map/reduce_scatter | solution.py:28
  129.4 1.6 fusion.17
  131.0 0.0 all-reduce.3.cloned.1.call-start
  131.0 59.8 %all-gather.2.cloned.1.call-done = bf16[4096,256]{1,0:T(8,128)(2,1)} async-done(((bf16[128,256]{1,0:T(8,128)(2,1)}), bf16[4096,256]{1,0:T(8,128)(2,1)}) %all-gather.2.cloned.1.call-update) | async-done | bytes 2097168 | tf_op jit(solution)/shard_map/all_gather | solution.py:34
  190.8 2.7 fusion.5
  193.5 2.7 fusion.8
  196.2 135.8 %all-reduce.3.cloned.1.call-done = (f32[32,256]{1,0:T(8,128)}, f32[32,256]{1,0:T(8,128)}) async-done(((f32[32,256]{1,0:T(8,128)}, f32[32,256]{1,0:T(8,128)}), (f32[32,256]{1,0:T(8,128)}, f32[32,256]{1,0:T(8,128)})) %all-reduce.3.cloned.1.call-update) | async-done | bytes 65552 | tf_op jit(solution)/shard_map/psum | solution.py:37
  332.0 1.4 copy.43
  333.4 1.4 copy.44
  (13 shorter events, 0.1 us)
Async XLA Ops:
  7.2 9.0 %copy-start = (bf16[32,256]{1,0:T(8,128)(2,1)S(1)}, bf16[32,256]{1,0:T(8,128)(2,1)}, u32[]{:S(2)}) copy-start(bf16[32,256]{1,0:T(8,128)(2,1)} %param.10) | copy-start | bytes 49156
  7.2 122.2 %reduce-scatter.2.cloned.1.call-start = ((), (), s32[]{:S(2)}) async-start(), calls=%async_computation.1 | async-start | bytes 4325376 | tf_op jit(solution)/shard_map/reduce_scatter | solution.py:28
  15.5 1.4 copy-start.2
  19.6 109.7 %copy-start.1 = (bf16[1,128,256]{2,1,0:T(8,128)(2,1)S(1)}, bf16[1,128,256]{2,1,0:T(8,128)(2,1)}, u32[]{:S(2)}) copy-start(bf16[1,128,256]{2,1,0:T(8,128)(2,1)} %param.17) | copy-start | bytes 196612
  19.6 109.7 %copy-start.3 = (f32[256]{0:T(256)S(1)}, f32[256]{0:T(256)}, u32[]{:S(2)}) copy-start(f32[256]{0:T(256)} %param.12) | copy-start | bytes 3076
  19.7 171.2 %all-gather.2.cloned.1.call-start = ((), (), s32[]{:S(2)}) async-start(), calls=%async_computation.2 | async-start | bytes 2162688 | tf_op jit(solution)/shard_map/all_gather | solution.py:34
  131.0 201.0 %all-reduce.3.cloned.1.call-start = ((), (), s32[]{:S(2)}) async-start(), calls=%async_computation.3 | async-start | bytes 131072 | tf_op jit(solution)/shard_map/psum | solution.py:37
Sparse Core Ops, SparseCore 0:
  19.8 109.5 reduce-scatter.1
  132.5 58.2 all-gather.1
  196.3 135.6 all-reduce.2
where the time goes:
time: 342 us; the launch traced here: 341 us
  waiting for transfers between devices  305 us (89%)
  between operations  13.8 us (4%)
  matrix products  11.9 us (3%)
  local copies, waits for them, and re-layouts  6.39 us (2%)
  other arithmetic  3.69 us (1%)
    psum x1, waiting for transfers between devices, body(): grad_self, grad_neigh = lax.psum((grad_self, grad_neigh), 'rep')  136 us
    reduce_scatter x1, waiting for transfers between devices, body(): lax.psum_scatter(partial_sums, 'feat', scatter_dimension=0, tiled=True)  110 us
    all_gather x1, waiting for transfers between devices, body(): pieces = lax.all_gather(output_grad, 'feat', axis=0, tiled=True)  59.8 us
  transfers between devices with their start and end apart: 3, of which 3 were waited for; matrix products, arithmetic and copies ran while one was open for 0% of the time, Pallas kernels for 0%

commit v1 on v0

--- a/solution.py
+++ b/solution.py
@@ -31,7 +31,9 @@
     output_grad = (
         cotangent[0].astype(jnp.float32) * squash * (1.0 + preact * (1.0 - squash))
     ).astype(jnp.bfloat16)
-    pieces = lax.all_gather(output_grad, "feat", axis=0, tiled=True)
+    pieces = jnp.concatenate(
+        lax.all_to_all(jnp.stack([output_grad] * lax.axis_size("feat")), "feat", 0, 0), axis=0
+    )
     grad_self = transposed_product(target_rows, pieces)
     grad_neigh = transposed_product(target_mean, pieces)
     grad_self, grad_neigh = lax.psum((grad_self, grad_neigh), "rep")

time: 342 us -> 311 us (0.909)
  waiting for transfers between devices: 305 us -> 246 us
  blocking collectives: 0 us -> 31.3 us
    all_gather x1 -> x0, waiting for transfers between devices: 59.8 us -> none  [body(): pieces = lax.all_gather(output_grad, 'feat', axis=0, tiled=True)]
    all_to_all x0 -> x1, blocking collectives: none -> 31.3 us  [body(): lax.all_to_all(jnp.stack([output_grad] * lax.axis_size('feat')), 'feat',...]
  transfers between devices with their start and end apart: 3 -> 2, of which waited for: 3 -> 2; matrix products, arithmetic and copies ran while one was open for 0% -> 0% of each run, Pallas kernels for 0% -> 0%
where the time goes in v1:
time: 311 us
  waiting for transfers between devices  246 us (79%)
  blocking collectives  31.3 us (10%)
  between operations  14.1 us (5%)
  matrix products  8.77 us (3%)
  local copies, waits for them, and re-layouts  6.62 us (2%)
  other arithmetic  3.68 us (1%)
    psum x1, waiting for transfers between devices, body(): grad_self, grad_neigh = lax.psum((grad_self, grad_neigh), 'rep')  136 us
    reduce_scatter x1, waiting for transfers between devices, body(): lax.psum_scatter(partial_sums, 'feat', scatter_dimension=0, tiled=True)  110 us
    all_to_all x1, blocking collectives, body(): lax.all_to_all(jnp.stack([output_grad] * lax.axis_size('feat')), 'feat',...  31.3 us
  transfers between devices with their start and end apart: 2, of which 2 were waited for; matrix products, arithmetic and copies ran while one was open for 0% of the time, Pallas kernels for 0%

profile of v1, /device:TPU:2, one launch (start us, length us, event | category | flops | bytes accessed | tf_op | source)
XLA Modules:
  0.0 310.6 jit_solution(13807582159321670160)
XLA Ops:
  7.2 0.0 reduce-scatter.2.cloned.1.call-start
  7.2 0.7 fusion.14
  7.9 0.7 compare_select_fusion
  8.6 0.7 iota_compare_fusion
  9.3 0.1 copy.19
  9.4 0.1 reshape.133
  9.5 1.2 copy.25
  10.7 0.3 copy.17
  11.0 0.6 gather_fusion
  11.6 0.7 gather_fusion.1
  12.4 3.2 %fusion.4 = bf16[32,128,32]{1,2,0:T(8,128)(2,1)S(1)} fusion(bf16[32,3,128,32]{2,3,1,0:T(8,128)(2,1)S(1)} %bitcast.60, bf16[1,32,3,128,128]{4,3,2,1,0:T(8,128)(2,1)} %param.13, pred[32,3]{1,0:T(8,128)(4,1)S(1)} %iota_compare_fusion), kind=kOutput, calls=%fused_computation.9 | convolution fusion | flops 102367232 | bytes 4194400 | tf_op jit(solution)/shard_map/bkij,bkjc->bic/dot_general | solution.py:21
  15.6 0.6 gather_fusion.2
  16.2 0.7 fusion.7
  16.9 2.7 convolution_add_fusion
  19.7 0.0 all-reduce.3.cloned.1.call-start
  19.7 109.6 %reduce-scatter.2.cloned.1.call-done = f32[128,256]{1,0:T(8,128)} async-done(((f32[4096,256]{1,0:T(8,128)}), f32[128,256]{1,0:T(8,128)}) %reduce-scatter.2.cloned.1.call-update) | async-done | bytes 131088 | tf_op jit(solution)/shard_map/reduce_scatter | solution.py:28
  129.4 1.6 fusion.11
  130.9 0.2 stack.2
  131.2 31.3 %all_to_all.5 = bf16[32,128,256]{2,1,0:T(8,128)(2,1)S(1)} all-to-all(bf16[32,128,256]{2,1,0:T(8,128)(2,1)S(1)} %stack.2), channel_id=1, replica_groups=mesh['feat'=32,'rep'=16] {'feat'}, dimensions={0} | all-to-all | bytes 4194304 | tf_op jit(solution)/shard_map/all_to_all | solution.py:35
  162.5 1.1 convolution_bitcast_fusion
  163.6 1.1 convolution_bitcast_fusion.1
  164.7 136.4 %all-reduce.3.cloned.1.call-done = (f32[32,256]{1,0:T(8,128)}, f32[32,256]{1,0:T(8,128)}) async-done(((f32[32,256]{1,0:T(8,128)}, f32[32,256]{1,0:T(8,128)}), (f32[32,256]{1,0:T(8,128)}, f32[32,256]{1,0:T(8,128)})) %all-reduce.3.cloned.1.call-update) | async-done | bytes 65552 | tf_op jit(solution)/shard_map/psum | solution.py:39
  301.0 1.4 copy.36
  302.4 1.4 copy.37
  (12 shorter events, 0.1 us)
Async XLA Ops:
  7.2 9.0 %copy-start = (bf16[32,256]{1,0:T(8,128)(2,1)S(1)}, bf16[32,256]{1,0:T(8,128)(2,1)}, u32[]{:S(2)}) copy-start(bf16[32,256]{1,0:T(8,128)(2,1)} %param.10) | copy-start | bytes 49156
  7.2 122.2 %reduce-scatter.2.cloned.1.call-start = ((), (), s32[]{:S(2)}) async-start(), calls=%async_computation.2 | async-start | bytes 4325376 | tf_op jit(solution)/shard_map/reduce_scatter | solution.py:28
  15.5 1.4 copy-start.2
  19.6 109.7 %copy-start.1 = (bf16[1,128,256]{2,1,0:T(8,128)(2,1)S(1)}, bf16[1,128,256]{2,1,0:T(8,128)(2,1)}, u32[]{:S(2)}) copy-start(bf16[1,128,256]{2,1,0:T(8,128)(2,1)} %param.17) | copy-start | bytes 196612
  19.6 109.7 %copy-start.3 = (f32[256]{0:T(256)S(1)}, f32[256]{0:T(256)}, u32[]{:S(2)}) copy-start(f32[256]{0:T(256)} %param.12) | copy-start | bytes 3076
  19.7 281.4 %all-reduce.3.cloned.1.call-start = ((), (), s32[]{:S(2)}) async-start(), calls=%async_computation.3 | async-start | bytes 131072 | tf_op jit(solution)/shard_map/psum | solution.py:39
Sparse Core Ops, SparseCore 0:
  19.8 109.5 reduce-scatter.1
  164.8 136.1 all-reduce.2
